TPU v7x, 256 devices: a whole 4x4x8 slice. The times are simulated.
256 devices in a mesh: col: 32 (over x, z_hi, core), row: 8 (over y, z_lo).
Axes of the slice: x: 4, y: 4, z: 8 (z_hi: 4, z_lo: 2; z = z_hi * 2 + z_lo), core: 2. Of those that a mesh axis runs over, the one named last changes fastest.
Arguments:
- weight: bfloat16 [8192, 53248], P('row', 'col'), may hold values from -6 to 6
- factor: float32 [1664, 53248], P('row', 'col'), may hold values from -1 to 2, as said below
- keep_mask: int32 [64, 13], P('row'), may hold values 0 or 1
Outputs:
- pruned: bfloat16 [8192, 53248], P('row', 'col')
Inputs may be any that keep to these rules, and one draw needn't show every extreme that they name: factor[i, k] = 0 for k < i; the diagonal entries factor[i, i] lie in [0.5, 2].
All inputs are finite; a program needn't handle non-finite values. No bound on the sum of `keep_mask` on one device may be relied on, other than what follows from the above.
Results may differ from a plain program's by a relative error of at most 0.0035.
Values may be sent and summed in bfloat16 or wider, within the bound.
No kernel may reach another device: no remote copies, remote signals or barrier semaphores. Data moves between devices by JAX's collectives and lax.ppermute only.
A program may use at most 192 MiB of HBM per device.

v0:
```python
from functools import partial
import jax
import jax.numpy as jnp
from jax import lax
from jax.sharding import PartitionSpec as P

PANW = 832
BLK = 128
PCOLS = 1664


def broadcast(x, axis, root):
    mine = lax.axis_index(axis) == root
    return lax.psum(jnp.where(mine, x, jnp.zeros_like(x)), axis)


def unit_inverse(strict, identity):
    width = strict.shape[0]
    result = identity - strict
    powered = strict
    reached = 2
    while reached < width:
        powered = jnp.dot(powered, powered, precision=lax.Precision.HIGHEST)
        result = jnp.dot(result, identity + powered, precision=lax.Precision.HIGHEST)
        reached = reached * 2
    return result


def prune_range(panel_state, keep_rows, diag_block, start_col, stop_col):
    sub_width = BLK // 2
    kept_parts = []
    error_parts = []
    identity = jnp.eye(sub_width, dtype=jnp.float32)
    for pan_start in range(start_col, stop_col, PANW):
        pan_stop = pan_start + PANW
        pieces = [
            panel_state[:, low : low + sub_width] for low in range(pan_start, pan_stop, sub_width)
        ]
        pan_errors = []
        for place in range(len(pieces)):
            sub_start = pan_start + place * sub_width
            sub_stop = sub_start + sub_width
            block_col = sub_start // BLK
            keep_col = jnp.repeat(
                keep_rows[:, block_col : block_col + 1].astype(jnp.float32), BLK, axis=0
            )
            dropped_col = 1.0 - keep_col
            columns = pieces[place]
            factor_sub = diag_block[sub_start:sub_stop, sub_start:sub_stop]
            pivots = jnp.diagonal(factor_sub)
            strict = jnp.triu(factor_sub, 1) / pivots[:, None]
            inverse = unit_inverse(strict, identity)
            solved = jnp.dot(columns, inverse, precision=lax.Precision.HIGHEST)
            current = jnp.where(dropped_col > 0.5, solved, columns)
            errors = dropped_col * current / pivots[None, :]
            kept_parts.append(keep_col * current)
            pan_errors.append(errors)
            if sub_stop < pan_stop:
                update = jnp.dot(
                    errors,
                    diag_block[sub_start:sub_stop, sub_stop:pan_stop],
                    precision=lax.Precision.HIGHEST,
                )
                for later in range(place + 1, len(pieces)):
                    offset = (later - place - 1) * sub_width
                    pieces[later] = pieces[later] - update[:, offset : offset + sub_width]
        pan_error = jnp.concatenate(pan_errors, axis=1)
        error_parts.append(pan_error)
        if pan_stop < PCOLS:
            later_update = jnp.dot(
                pan_error,
                diag_block[pan_start:pan_stop, pan_stop:],
                precision=lax.Precision.HIGHEST,
            )
            panel_state = jnp.concatenate(
                [panel_state[:, :pan_stop], panel_state[:, pan_stop:] - later_update], axis=1
            )
    return (panel_state, jnp.concatenate(kept_parts, axis=1), jnp.concatenate(error_parts, axis=1))


def skip_range(panel_state, keep_rows, diag_block, start_col, stop_col):
    blank = jnp.zeros((panel_state.shape[0], stop_col - start_col), jnp.float32)
    return (panel_state, blank, blank)


def per_device(weight, factor, keep_mask):
    section = lax.axis_index("col")
    owner = section == 0
    gathered = lax.all_gather(factor, "row", axis=0, tiled=True)
    factor_low = gathered.astype(jnp.bfloat16)
    panel_state = weight.astype(jnp.float32)
    panel_state, kept, error_all = lax.cond(
        owner,
        partial(prune_range, start_col=0, stop_col=PCOLS),
        partial(skip_range, start_col=0, stop_col=PCOLS),
        panel_state,
        keep_mask,
        gathered,
    )
    arrived = broadcast(error_all.astype(jnp.bfloat16), "col", 0)
    compensation = jnp.dot(arrived, factor_low, preferred_element_type=jnp.float32)
    section_width = weight.shape[1]
    global_cols = section * section_width + jnp.arange(section_width, dtype=jnp.int32)
    kept_padded = jnp.concatenate(
        [kept, jnp.zeros((kept.shape[0], section_width - PCOLS), jnp.float32)], axis=1
    )
    trailing = weight.astype(jnp.float32) - compensation
    return jnp.where((global_cols < PCOLS)[None, :], kept_padded, trailing).astype(jnp.bfloat16)


def solution(mesh):
    in_specs = (P("row", "col"), P("row", "col"), P("row", None))
    out_specs = P("row", "col")
    return jax.shard_map(
        per_device, mesh=mesh, in_specs=in_specs, out_specs=out_specs, check_vma=False
    )
```

profile of v0, /device:TPU:1, one launch (start us, length us, event | category | flops | bytes accessed | tf_op | source)
XLA Modules:
  0.0 870.4 jit_solution(3260335162966329133)
XLA Ops:
  6.5 0.0 all-gather.2.cloned.1.call-start
  6.5 0.7 all-gather.2.cloned.1.call-update
  7.3 0.0 all-reduce.2.cloned.1.call-start
  7.3 0.0 copy-start.64
  7.3 5.1 convert_element_type.409
  12.4 221.6 %all-gather.2.cloned.1.call-done = f32[1664,1664]{1,0:T(8,128)} async-done(((f32[208,1664]{1,0:T(8,128)}), f32[1664,1664]{1,0:T(8,128)}) %all-gather.2.cloned.1.call-update) | async-done | bytes 11075600 | tf_op jit(solution)/shard_map/all_gather | solution.py:89
  234.1 0.0 copy-done.64
  234.1 4.2 conditional.1
  234.1 2.2 broadcast.398
  236.3 2.0 broadcast.397.clone
  238.2 1.9 broadcast_select_fusion
  240.2 0.0 copy-start.6
  240.2 0.0 all-reduce.2.cloned.1.call-update
  240.2 609.3 %all-reduce.2.cloned.1.call-done = bf16[1024,1664]{0,1:T(8,128)(2,1)} async-done(((bf16[1024,1664]{0,1:T(8,128)(2,1)}), bf16[1024,1664]{0,1:T(8,128)(2,1)}) %all-reduce.2.cloned.1.call-update) | async-done | bytes 3407888 | tf_op jit(solution)/shard_map/psum | solution.py:14
  849.5 0.0 copy-done.6
  849.6 14.0 %select_convert_fusion = bf16[1024,1664]{1,0:T(8,128)(2,1)} fusion(bf16[1024,1664]{1,0:T(8,128)(2,1)} %get-tuple-element.27, pred[1664]{0:T(1024)(128)(4,1)S(1)} %add_compare_fusion, bf16[1024,1664]{0,1:T(8,128)(2,1)} %all-reduce.2.cloned.1.call-done, f32[1664,1664]{1,0:T(8,128)} %all-gather.2.cloned.1.call-done, bf16[1024,1664]{1,0:T(8,128)(2,1)S(1)} %copy-done.6), kind=kOutput, calls=%fused_computation.857 | convolution fusion | flops 5678579712 | bytes 24708736 | tf_op jit(solution)/shard_map/dot_general | solution.py:101
  (1 shorter events, 0.0 us)
Async XLA Ops:
  6.5 227.5 %all-gather.2.cloned.1.call-start = ((), (), s32[]{:S(2)}) async-start(), calls=%async_computation | async-start | bytes 12460032 | tf_op jit(solution)/shard_map/all_gather | solution.py:89
  7.3 842.3 %all-reduce.2.cloned.1.call-start = ((), (), s32[]{:S(2)}) async-start(), calls=%async_computation.1 | async-start | bytes 6815744 | tf_op jit(solution)/shard_map/psum | solution.py:14
  7.3 226.8 %copy-start.64 = (s32[8,13]{1,0:T(8,128)S(1)}, s32[8,13]{1,0:T(8,128)}, u32[]{:S(2)}) copy-start(s32[8,13]{1,0:T(8,128)} %param.7) | copy-start | bytes 1252
  240.2 609.4 %copy-start.6 = (bf16[1024,1664]{1,0:T(8,128)(2,1)S(1)}, bf16[1024,1664]{1,0:T(8,128)(2,1)}, u32[]{:S(2)}) copy-start(bf16[1024,1664]{1,0:T(8,128)(2,1)} %param.5) | copy-start | bytes 10223620
Sparse Core Ops, SparseCore 0:
  9.1 224.9 all-gather.1
  240.3 609.1 all-reduce.1
where the time goes:
time: 886 us; the launch traced here: 870 us
  waiting for transfers between devices  832 us (94%)
  matrix products  14 us (2%)
  between operations  13.4 us (2%)
    psum x1, waiting for transfers between devices, broadcast(): return lax.psum(jnp.where(mine, x, jnp.zeros_like(x)), axis)  609 us
    all_gather x1, waiting for transfers between devices, per_device(): gathered = lax.all_gather(factor, 'row', axis=0, tiled=True)  222 us
  transfers between devices with their start and end apart: 2, of which 2 were waited for; matrix products, arithmetic and copies ran while one was open for 1% of the time, Pallas kernels for 0%

commit v1 on v0

--- a/solution.py
+++ b/solution.py
@@ -86,7 +86,9 @@
 def per_device(weight, factor, keep_mask):
     section = lax.axis_index("col")
     owner = section == 0
-    gathered = lax.all_gather(factor, "row", axis=0, tiled=True)
+    gathered = jnp.concatenate(
+        lax.all_to_all(jnp.stack([factor] * lax.axis_size("row")), "row", 0, 0), axis=0
+    )
     factor_low = gathered.astype(jnp.bfloat16)
     panel_state = weight.astype(jnp.float32)
     panel_state, kept, error_all = lax.cond(

time: 886 us -> 786 us (0.89)
  waiting for transfers between devices: 832 us -> 728 us
    all_gather x1 -> x0, waiting for transfers between devices: 222 us -> none  [per_device(): gathered = lax.all_gather(factor, 'row', axis=0, tiled=True)]
    all_to_all x0 -> x1, waiting for transfers between devices: none -> 118 us  [per_device(): lax.all_to_all(jnp.stack([factor] * lax.axis_size('row')), 'row', 0, 0)]
  transfers between devices with their start and end apart: 2 -> 2, of which waited for: 2 -> 2; matrix products, arithmetic and copies ran while one was open for 1% -> 0% of each run, Pallas kernels for 0% -> 0%
where the time goes in v1:
time: 786 us; the launch traced here: 777 us
  waiting for transfers between devices  728 us (93%)
  matrix products  14 us (2%)
  between operations  13.4 us (2%)
  local copies, waits for them, and re-layouts  10.2 us (1%)
    psum x1, waiting for transfers between devices, broadcast(): return lax.psum(jnp.where(mine, x, jnp.zeros_like(x)), axis)  609 us
    all_to_all x1, waiting for transfers between devices, per_device(): lax.all_to_all(jnp.stack([factor] * lax.axis_size('row')), 'row', 0, 0)  118 us
  transfers between devices with their start and end apart: 2, of which 2 were waited for; matrix products, arithmetic and copies ran while one was open for 0% of the time, Pallas kernels for 0%

profile of v1, /device:TPU:1, one launch (start us, length us, event | category | flops | bytes accessed | tf_op | source)
XLA Modules:
  0.0 777.2 jit_solution(2731687882761739966)
XLA Ops:
  6.5 6.1 stack.2
  12.6 0.0 copy-start.6
  12.6 6.6 all-to-all-start
  19.3 0.0 all-reduce.2.cloned.1.call-start
  19.3 0.0 copy-done.6
  19.3 0.0 copy-start.65
  19.3 3.3 convert_element_type.409
  22.6 118.3 %all-to-all-done = f32[8,208,1664]{2,1,0:T(8,128)} async-done(((f32[8,208,1664]{2,1,0:T(8,128)}), f32[8,208,1664]{2,1,0:T(8,128)}, u32[]{:S(2)}, u32[]{:S(2)}) %all-to-all-start) | async-done | bytes 11075616 | tf_op jit(solution)/shard_map/all_to_all | solution.py:90
  140.9 0.0 copy-done.65
  140.9 4.1 conditional.1
  140.9 2.1 broadcast.400
  143.0 2.0 broadcast.399.clone
  145.0 1.9 broadcast_select_fusion
  147.0 0.0 copy-start.7
  147.0 0.0 all-reduce.2.cloned.1.call-update
  147.0 609.3 %all-reduce.2.cloned.1.call-done = bf16[1024,1664]{0,1:T(8,128)(2,1)} async-done(((bf16[1024,1664]{0,1:T(8,128)(2,1)}), bf16[1024,1664]{0,1:T(8,128)(2,1)}) %all-reduce.2.cloned.1.call-update) | async-done | bytes 3407888 | tf_op jit(solution)/shard_map/psum | solution.py:14
  756.3 0.0 copy-done.7
  756.3 14.0 %select_convert_fusion = bf16[1024,1664]{1,0:T(8,128)(2,1)} fusion(bf16[1024,1664]{1,0:T(8,128)(2,1)} %get-tuple-element.27, pred[1664]{0:T(1024)(128)(4,1)S(1)} %add_compare_fusion, bf16[1024,1664]{0,1:T(8,128)(2,1)} %all-reduce.2.cloned.1.call-done, f32[1664,1664]{1,0:T(8,128)} %bitcast.28, bf16[1024,1664]{1,0:T(8,128)(2,1)S(1)} %copy-done.7), kind=kOutput, calls=%fused_computation.857 | convolution fusion | flops 5678579712 | bytes 24708736 | tf_op jit(solution)/shard_map/dot_general | solution.py:103
  (1 shorter events, 0.0 us)
Async XLA Ops:
  12.6 6.7 copy-start.6
  12.6 128.3 %all-to-all-start = ((f32[8,208,1664]{2,1,0:T(8,128)}), f32[8,208,1664]{2,1,0:T(8,128)}, u32[]{:S(2)}, u32[]{:S(2)}) async-start(f32[8,208,1664]{2,1,0:T(8,128)} %stack.2), calls=%async_computation | async-start | bytes 22151168 | tf_op jit(solution)/shard_map/all_to_all | solution.py:90
  19.3 737.0 %all-reduce.2.cloned.1.call-start = ((), (), s32[]{:S(2)}) async-start(), calls=%async_computation.1 | async-start | bytes 6815744 | tf_op jit(solution)/shard_map/psum | solution.py:14
  19.3 121.6 %copy-start.65 = (s32[8,13]{1,0:T(8,128)S(1)}, s32[8,13]{1,0:T(8,128)}, u32[]{:S(2)}) copy-start(s32[8,13]{1,0:T(8,128)} %param.7) | copy-start | bytes 1252
  147.0 609.3 %copy-start.7 = (bf16[1024,1664]{1,0:T(8,128)(2,1)S(1)}, bf16[1024,1664]{1,0:T(8,128)(2,1)}, u32[]{:S(2)}) copy-start(bf16[1024,1664]{1,0:T(8,128)(2,1)} %param.5) | copy-start | bytes 10223620
Sparse Core Ops, SparseCore 0:
  147.1 609.1 all-reduce.1
